TPU v7x, 128 devices: a whole 4x4x4 slice. The times are simulated.
128 devices in a mesh: dp: 4 (over x), seq: 32 (over z, y, core).
Axes of the slice: x: 4, y: 4, z: 4, core: 2. Of those that a mesh axis runs over, the one named last changes fastest.
Arguments:
- conv_input: bfloat16 [16384, 5376], P(('dp', 'seq')), may hold values from -6 to 6
- doc_start: int32 [16384], P(('dp', 'seq')), may hold values 0 or 1
- conv_weight: float32 [4, 5376], replicated, may hold values from -3 to 3
- conv_bias: float32 [5376], replicated, may hold values from -0.5 to 0.5
- dt_raw: float32 [16384, 80], P(('dp', 'seq')), may hold values from -3 to 3
- dt_bias: float32 [80], replicated, may hold values from -5.5 to -4.2
- a_log: float32 [80], replicated, may hold values from -9 to 2, as said below
- skip_gain: float32 [80], replicated, may hold values from 0.5 to 1.5
- cotangent: bfloat16 [16384, 5120], P(('dp', 'seq')), may hold values from -6 to 6
Outputs:
- ssm_output: bfloat16 [16384, 5120], P(('dp', 'seq'))
- grad_input: bfloat16 [16384, 5376], P(('dp', 'seq'))
- grad_conv_weight: float32 [4, 5376], replicated
- grad_conv_bias: float32 [5376], replicated
- grad_dt_bias: float32 [80], replicated
- grad_a_log: float32 [80], replicated
- grad_skip_gain: float32 [80], replicated
Inputs may be any that keep to these rules, and one draw needn't show every extreme that they name: `doc_start`: 1 marks the first token of a document; documents may cross shard boundaries. One value per head; exp(a_log) lies between 25 / 4096 and 4.2, so that the per-token decay rates exp(a_log) * steps_dt run from under 1 / 4096 to about 1.1.
All inputs are finite; a program needn't handle non-finite values.
Results may differ from a plain program's by a relative error of at most 0.00115.
Values may be sent and summed in bfloat16 or wider, within the bound.
A program may use at most 320 MiB of HBM per device.

v0:
```python
import jax
import jax.numpy as jnp
from jax import lax
from jax.sharding import PartitionSpec as P

HEADS = 80
HEAD_DIM = 64
STATE = 128
CONV = 4
BLOCK = 64
INNER = 5120
exact_mode = lax.Precision.HIGHEST


def from_behind(array, axis, by):
    size = lax.axis_size(axis)
    pairs = [(i, i + by) for i in range(size) if 0 <= i + by < size]
    return lax.ppermute(array, axis, pairs)


def prefix(array, axis, combine, identity, reverse):
    size, place = (lax.axis_size(axis), lax.axis_index(axis))
    everything = jax.tree.map(lambda part: lax.all_gather(part, axis), array)
    start = jax.tree.map(
        lambda part, zero: jnp.broadcast_to(jnp.asarray(zero, part.dtype), part.shape),
        array,
        identity,
    )

    def step(k, before):
        at = size - 1 - k if reverse else k
        reached = at > place if reverse else at < place
        new = combine(before, jax.tree.map(lambda part: part[at], everything))
        return jax.tree.map(lambda a, b: jnp.where(reached, a, b), new, before)

    return lax.fori_loop(0, size, step, start)


def prepare_inputs(
    tail_rows, conv_input, doc_start, conv_weight, conv_bias, dt_raw, dt_bias, a_log
):
    row_count = conv_input.shape[0]
    extended = jnp.concatenate([tail_rows, conv_input], axis=0)
    resets = doc_start.astype(jnp.float32)
    segment = jnp.cumsum(resets)
    padded = jnp.concatenate([jnp.zeros((CONV - 1,), jnp.float32), segment])
    convolved = conv_bias[None, :] + conv_weight[CONV - 1][None, :] * extended[CONV - 1 :]
    for offset in range(1, CONV):
        first_row = CONV - 1 - offset
        tap_valid = (padded[first_row : first_row + row_count] == segment).astype(jnp.float32)
        convolved = (
            convolved
            + conv_weight[first_row][None, :]
            * extended[first_row : first_row + row_count]
            * tap_valid[:, None]
        )
    activated = jax.nn.silu(convolved)
    values_x = activated[:, :INNER].reshape(row_count, HEADS, HEAD_DIM)
    keys_b = activated[:, INNER : INNER + STATE]
    reads_c = activated[:, INNER + STATE :]
    steps_dt = jax.nn.softplus(dt_raw + dt_bias[None, :])
    log_decay = -jnp.exp(a_log)[None, :] * steps_dt
    return (values_x, keys_b, reads_c, steps_dt, log_decay)


def scan_block(carry, block_data):
    carry_state, skip_gain = carry
    values_x, keys_b, reads_c, steps_dt, log_decay, resets = block_data
    length = values_x.shape[0]
    segment = jnp.cumsum(resets)
    running = jnp.cumsum(log_decay, axis=0)
    positions = jnp.arange(length)
    causal = (positions[:, None] >= positions[None, :]) & (segment[:, None] == segment[None, :])
    spread_log = running.T[:, :, None] - running.T[:, None, :]
    within = jnp.where(causal[None], jnp.exp(jnp.where(causal[None], spread_log, 0.0)), 0.0)
    scores = jnp.dot(reads_c, keys_b.T, precision=exact_mode)
    weights = within * scores[None] * steps_dt.T[:, None, :]
    output = jnp.einsum("hts,shp->thp", weights, values_x, precision=exact_mode)
    untouched = (segment == 0).astype(running.dtype)
    entry_weight = jnp.exp(running) * untouched[:, None]
    output = (
        output
        + jnp.einsum("tn,hpn->thp", reads_c, carry_state, precision=exact_mode)
        * entry_weight[:, :, None]
    )
    output = output + skip_gain[None, :, None] * values_x
    last_segment = (segment == segment[length - 1]).astype(running.dtype)
    leave_weight = (
        jnp.exp(running[length - 1][None, :] - running) * last_segment[:, None] * steps_dt
    )
    through = jnp.exp(running[length - 1]) * untouched[length - 1]
    added = jnp.einsum(
        "shp,sn->hpn", leave_weight[:, :, None] * values_x, keys_b, precision=exact_mode
    )
    carry_state = carry_state * through[:, None, None] + added
    return ((carry_state, skip_gain), output)


def chain_blocks(values_x, keys_b, reads_c, steps_dt, log_decay, resets, skip_gain, start_state):
    row_count = values_x.shape[0]
    block_count = row_count // BLOCK
    pieces = tuple(
        (
            member.reshape((block_count, BLOCK) + member.shape[1:])
            for member in (values_x, keys_b, reads_c, steps_dt, log_decay, resets)
        )
    )
    stepper = jax.checkpoint(scan_block)
    (final_state, _), outputs = lax.scan(stepper, (start_state, skip_gain), pieces)
    return (outputs.reshape(row_count, INNER), final_state)


def join_states(earlier, later):
    return (earlier[0] * later[0], later[0][:, None, None] * earlier[1] + later[1])


def on_device(
    conv_input, doc_start, conv_weight, conv_bias, dt_raw, dt_bias, a_log, skip_gain, cotangent
):
    row_count = conv_input.shape[0]
    resets = doc_start.astype(jnp.float32)
    after = jnp.concatenate([1.0 - resets[row_count - CONV + 2 :], jnp.ones((1,), jnp.float32)])
    keep_rows = jnp.flip(jnp.cumprod(jnp.flip(after)))
    tail_out = conv_input[row_count - CONV + 1 :] * keep_rows[:, None].astype(jnp.bfloat16)
    tail_in = from_behind(tail_out, "seq", 1)

    def prepare_local(tail_rows, rows_value, weight_value, bias_value, dtb_value, alog_value):
        return prepare_inputs(
            tail_rows,
            rows_value,
            doc_start,
            weight_value,
            bias_value,
            dt_raw,
            dtb_value,
            alog_value,
        )

    prepared, pull_prep = jax.vjp(
        prepare_local,
        tail_in.astype(jnp.float32),
        conv_input.astype(jnp.float32),
        conv_weight,
        conv_bias,
        dt_bias,
        a_log,
    )
    values_x, keys_b, reads_c, steps_dt, log_decay = prepared
    zero_state = jnp.zeros((HEADS, HEAD_DIM, STATE), jnp.float32)

    def local_chain(x_value, b_value, c_value, dt_value, decay_value, gain_value):
        return chain_blocks(
            x_value, b_value, c_value, dt_value, decay_value, resets, gain_value, zero_state
        )

    (local_out, local_state), pull_chain = jax.vjp(
        local_chain, values_x, keys_b, reads_c, steps_dt, log_decay, skip_gain
    )

    def entering(decay_value):
        running = jnp.cumsum(decay_value, axis=0)
        untouched = (jnp.cumsum(resets) == 0).astype(running.dtype)
        return (
            jnp.exp(running) * untouched[:, None],
            jnp.exp(running[row_count - 1]) * untouched[row_count - 1],
        )

    entry_weight, through = entering(log_decay)
    upstream = cotangent.astype(jnp.float32)
    upstream_heads = upstream.reshape(row_count, HEADS, HEAD_DIM)
    adjoint_local = jnp.einsum(
        "thp,tn->hpn", upstream_heads * entry_weight[:, :, None], reads_c, precision=exact_mode
    )
    identity = (jnp.ones((HEADS,), jnp.float32), jnp.zeros((HEADS, HEAD_DIM, STATE), jnp.float32))
    incoming = prefix((through, local_state), "seq", join_states, identity, False)[1]
    adjoint_end = prefix((through, adjoint_local), "seq", join_states, identity, True)[1]

    def carried(c_value, decay_value):
        weight_in, through_in = entering(decay_value)
        added = (
            jnp.einsum("tn,hpn->thp", c_value, incoming, precision=exact_mode)
            * weight_in[:, :, None]
        )
        return (added.reshape(row_count, INNER), through_in[:, None, None] * incoming)

    (carried_out, _), pull_carried = jax.vjp(carried, reads_c, log_decay)
    output = (local_out + carried_out).astype(jnp.bfloat16)
    grad_x, grad_b, grad_c, grad_dt, grad_decay, grad_gain = pull_chain((upstream, adjoint_end))
    grad_c_extra, grad_decay_extra = pull_carried((upstream, adjoint_end))
    grad_tail, grad_rows, grad_weight, grad_bias, grad_dtb, grad_alog = pull_prep(
        (grad_x, grad_b, grad_c + grad_c_extra, grad_dt, grad_decay + grad_decay_extra)
    )
    returned = from_behind(grad_tail, "seq", -1)
    grad_rows = jnp.concatenate(
        [
            grad_rows[: row_count - CONV + 1],
            grad_rows[row_count - CONV + 1 :] + returned * keep_rows[:, None],
        ],
        axis=0,
    )
    summed = lax.psum((grad_weight, grad_bias, grad_dtb, grad_alog, grad_gain), ("dp", "seq"))
    scale = float(lax.axis_size("dp") * lax.axis_size("seq") * row_count) ** (-0.5)
    return (
        output,
        grad_rows.astype(jnp.bfloat16),
        summed[0] * scale,
        summed[1] * scale,
        summed[2] * scale,
        summed[3] * scale,
        summed[4] * scale,
    )


def solution(mesh):
    return jax.shard_map(
        on_device,
        mesh=mesh,
        in_specs=(
            P(("dp", "seq"), None),
            P(("dp", "seq")),
            P(),
            P(),
            P(("dp", "seq"), None),
            P(),
            P(),
            P(),
            P(("dp", "seq"), None),
        ),
        out_specs=(P(("dp", "seq"), None), P(("dp", "seq"), None), P(), P(), P(), P(), P()),
        check_vma=False,
    )
```

profile of v0, /device:TPU:1, one launch (start us, length us, event | category | flops | bytes accessed | tf_op | source)
XLA Modules:
  0.0 1133.3 jit_solution(11397604116379961711)
XLA Ops:
  21.4 7.5 fusion.100
  36.5 69.3 %while.76 = (s32[]{:T(128)}, f32[80,64,128]{2,1,0:T(8,128)S(1)}, f32[2,64,80,64]{3,2,1,0:T(8,128)}, f32[2,80,64,128]{3,2,1,0:T(8,128)}, f32[2,80]{1,0:T(2,128)S(...) while((s32[]{:T(128)}, f32[80,64,128]{2,1,0:T(8,128)S(1)}, ...), condition=%wide.region_5.6_spmd.clone, body=%wide.region_2.5_spmd.clone.sunk | while | flops 1271495936 | bytes 43904780 | solution.py:109
  55.8 8.7 fusion.194
  90.4 8.7 fusion.194
  114.3 21.7 %all-gather.2 = f32[32,1,80]{2,1,0:T(1,128)S(1)} all-gather(f32[1,1,80]{2,1,0:T(1,128)S(1)} %multiply_bitcast_fusion), channel_id=1, replica_groups=mesh['dp'=4,'seq'=32] {'seq'}, dimensions={0}, use_global_device_ids=true | all-gather | bytes 10560 | tf_op jit(solution)/shard_map/all_gather | solution.py:23
  136.0 218.2 %all-gather.6.cloned.1.call-done = f32[2560,64,128]{2,1,0:T(8,128)} async-done(((f32[80,64,128]{2,1,0:T(8,128)}), f32[2560,64,128]{2,1,0:T(8,128)}) %all-gather.6.cloned.1.call-update) | async-done | bytes 83886096 | tf_op jit(solution)/shard_map/all_gather | solution.py:23
  354.3 77.1 %while.77 = (s32[]{:T(128)}, f32[80,64,128]{2,1,0:T(8,128)S(1)}, s32[]{:T(128)}, f32[32,80]{1,0:T(8,128)S(1)}, f32[32,80,64,128]{3,2,1,0:T(8,128)}, /*index=5*/s32[]{:T(128)}, s32[]{:T(128)}) while((s32[]{:T(128)}, f32[80,64,128]{2,1,0:T(8,128)S(1)}, s32[]{:T(128)}, f32[32,80]{1,0:T(8,128)S(1)}, f32[32,80,64,128]{3,2,1,0:T(8,128)}, ...), condition=%wide.region_8.9_spmd.clone, body=%wide.region_7.8_spmd.clone.sunk | while | flops 2621444 | bytes 7865393 | solution.py:36
  431.3 8.7 multiply_reduce_fusion.10
  452.7 8.1 copy.125
  460.8 6.5 copy.124
  484.9 205.6 %all-gather.8.cloned.1.call-done = f32[2560,64,128]{2,1,0:T(8,128)} async-done(((f32[80,64,128]{2,1,0:T(8,128)}), f32[2560,64,128]{2,1,0:T(8,128)}) %all-gather.8.cloned.1.call-update) | async-done | bytes 83886096 | tf_op jit(solution)/shard_map/all_gather | solution.py:23
  690.5 77.1 %while.78 = (s32[]{:T(128)}, f32[80,64,128]{2,1,0:T(8,128)S(1)}, s32[]{:T(128)}, f32[32,80]{1,0:T(8,128)S(1)}, f32[32,80,64,128]{3,2,1,0:T(8,128)}, /*index=5*/s32[]{:T(128)}, s32[]{:T(128)}, s32[]{:T(128)}, s32[]{:T(128)}) while((s32[]{:T(128)}, f32[80,64,128]{2,1,0:T(8,128)S(1)}, s32[]{:T(128)}, f32[32,80]{1,0:T(8,128)S(1)}, ...), condition=%wide.region_10.11_spmd.clone, body=%wide.region_9.10_spmd.clone.sunk | while | flops 2621448 | bytes 7865455 | solution.py:36
  772.6 176.0 %while.79 = (s32[]{:T(128)}, f32[80,64,128]{2,1,0:T(8,128)}, f32[80]{0:T(128)S(1)}, f32[2,64,80,64]{2,1,3,0:T(8,128)}, f32[2,64,128]{2,1,0:T(8,128)S(1)}, /*inde...) while((s32[]{:T(128)}, f32[80,64,128]{2,1,0:T(8,128)}, ...), condition=%wide.region_24.25_spmd.clone, body=%wide.region_11.24_spmd.clone.sunk | while | flops 3052656640 | bytes 114250048 | solution.py:109
  788.9 8.2 fusion.220
  797.3 9.1 multiply_reduce_fusion.17
  811.5 9.6 multiply_reduce_fusion.16
  836.9 6.5 fusion.219
  873.0 8.2 fusion.220
  881.4 9.1 multiply_reduce_fusion.17
  895.6 9.6 multiply_reduce_fusion.16
  921.2 6.5 fusion.219
  960.3 7.3 fusion.110
  986.6 66.0 %all-reduce.15 = (f32[5376]{0:T(1024)S(1)}, f32[80]{0:T(128)S(1)}, f32[80]{0:T(128)S(1)}, f32[80]{0:T(128)S(1)}) all-reduce(f32[5376]{0:T(1024)S(1)} %get-tuple-element.978, f32[80]{0:T(128)S(1)} %get-tuple-element.981, f32[80]{0:T(128)S(1)} %negate_multiply_fusion, ...), channel_id=1, replica_groups=mesh['dp'=4,'seq'=32] {'dp','seq'}, use_global_device_ids=true, to_apply=%region_31.32 | all-reduce | flops 5616 | bytes 44928 | tf_op jit(solution)/shard_map/psum | solution.py:201
  1057.0 65.2 %all-reduce.18.cloned.1.call-done = f32[4,5376]{1,0:T(4,128)} async-done(((f32[4,5376]{1,0:T(4,128)}), f32[4,5376]{1,0:T(4,128)}) %all-reduce.18.cloned.1.call-update) | async-done | bytes 86032 | tf_op jit(solution)/shard_map/psum | solution.py:201
  (465 shorter events, 407.7 us)
Async XLA Ops:
  7.2 14.3 %copy-start.37 = (f32[5376]{0:T(1024)S(1)}, f32[5376]{0:T(1024)}, u32[]{:S(2)}) copy-start(f32[5376]{0:T(1024)} %param.20) | copy-start | bytes 64516
  7.2 347.1 %all-gather.6.cloned.1.call-start = ((), (), s32[]{:S(2)}) async-start(), calls=%async_computation.1 | async-start | bytes 86507520 | tf_op jit(solution)/shard_map/all_gather | solution.py:23
  9.4 12.0 %collective-permute-start = (bf16[3,5376]{1,0:T(4,128)(2,1)S(1)}, bf16[3,5376]{1,0:T(4,128)(2,1)S(1)}, u32[]{:S(2)}, u32[]{:S(2)}) collective-permute-start(bf16[3,5376]{1,0:T(4,128)(2,1)S(1)} %slice_multiply_fusion), channel_id=1, source_target_pairs={{0,1},{1,2},{2,3},{3,4},{4,5},{5,6},{6,7},{7,8},{8,9},{9,10},{10,1... | collective-permute-start | bytes 96776 | tf_op jit(solution)/shard_map/ppermute | solution.py:18
  14.9 14.0 %copy-start.26 = (f32[128,80]{1,0:T(8,128)}, f32[128,80]{1,0:T(8,128)S(1)}, u32[]{:S(2)}) copy-start(f32[128,80]{1,0:T(8,128)S(1)} %copy.111) | copy-start | bytes 122884
  16.1 12.8 %copy-start.39 = (f32[128]{0:T(128)}, f32[128]{0:T(128)S(1)}, u32[]{:S(2)}) copy-start(f32[128]{0:T(128)S(1)} %get-tuple-element.1103) | copy-start | bytes 1540
  16.1 12.8 %copy-start.41 = (f32[128]{0:T(128)}, f32[128]{0:T(128)S(1)}, u32[]{:S(2)}) copy-start(f32[128]{0:T(128)S(1)} %get-tuple-element.1104) | copy-start | bytes 1540
  16.1 12.9 %copy-start.43 = (f32[128]{0:T(128)}, f32[128]{0:T(128)S(1)}, u32[]{:S(2)}) copy-start(f32[128]{0:T(128)S(1)} %get-tuple-element.1105) | copy-start | bytes 1540
  16.1 97.4 %copy-start.45 = (f32[128]{0:T(128)}, f32[128]{0:T(128)S(1)}, u32[]{:S(2)}) copy-start(f32[128]{0:T(128)S(1)} %get-tuple-element.1102) | copy-start | bytes 1540
  18.1 10.8 copy-start.29
  18.1 10.8 copy-start.31
  18.2 10.8 copy-start.33
  18.2 10.8 copy-start.35
  21.4 7.6 copy-start.22
  107.3 583.2 %all-gather.8.cloned.1.call-start = ((), (), s32[]{:S(2)}) async-start(), calls=%async_computation.2 | async-start | bytes 86507520 | tf_op jit(solution)/shard_map/all_gather | solution.py:23
  112.9 241.4 %copy-start.24 = (f32[128,80]{1,0:T(8,128)}, f32[128,80]{1,0:T(8,128)S(1)}, u32[]{:S(2)}) copy-start(f32[128,80]{1,0:T(8,128)S(1)} %reduce_window_sum.84) | copy-start | bytes 122884
  431.3 8.7 copy-start.5
  446.6 675.6 %all-reduce.18.cloned.1.call-start = ((), (), s32[]{:S(2)}) async-start(), calls=%async_computation | async-start | bytes 172032 | tf_op jit(solution)/shard_map/psum | solution.py:201
  797.3 9.1 copy-start
  881.3 9.1 copy-start
  954.8 12.9 %copy-start.23 = (f32[3,5376]{1,0:T(4,128)S(1)}, f32[3,5376]{1,0:T(4,128)}, u32[]{:S(2)}) copy-start(f32[3,5376]{1,0:T(4,128)} %copy-done.22) | copy-start | bytes 193540
  960.3 7.4 copy-start.40
  981.0 142.8 %copy-start.13 = (f32[128,5376]{1,0:T(8,128)S(1)}, f32[128,5376]{1,0:T(8,128)}, u32[]{:S(2)}) copy-start(f32[128,5376]{1,0:T(8,128)} %copy-done.12) | copy-start | bytes 8257540
  981.0 142.8 %copy-start.51 = (f32[3]{0:T(128)S(1)}, f32[3]{0:T(128)}, u32[]{:S(2)}) copy-start(f32[3]{0:T(128)} %copy-done.50) | copy-start | bytes 40
  981.0 142.8 %collective-permute-start.1 = (f32[3,5376]{1,0:T(4,128)S(1)}, f32[3,5376]{1,0:T(4,128)S(1)}, u32[]{:S(2)}, u32[]{:S(2)}) collective-permute-start(f32[3,5376]{1,0:T(4,128)S(1)} %pad_add_fusion.1), channel_id=1, source_target_pairs={{1,0},{2,1},{3,2},{4,3},{5,4},{6,5},{7,6},{8,7},{9,8},{10,9},{11,1... | collective-permute-start | bytes 193544 | tf_op jit(solution)/shard_map/ppermute | solution.py:18
  (41 other events, 188.7 us)
Sparse Core Ops, SparseCore 0:
  107.4 246.8 all-gather.5
  446.8 243.7 all-gather.7
  984.7 137.4 all-reduce.17
where the time goes:
time: 1140 us; the launch traced here: 1130 us
  waiting for transfers between devices  489 us (43%)
  other arithmetic  218 us (19%)
  matrix products  153 us (13%)
  local copies, waits for them, and re-layouts  151 us (13%)
  blocking collectives  87.7 us (8%)
  between operations  14.8 us (1%)
  loops' own time  12 us (1%)
    all_gather x2, waiting for transfers between devices, prefix(): everything = jax.tree.map(lambda part: lax.all_gather(part, axis), array)  424 us
    select_n x64, other arithmetic, step(): return jax.tree.map(lambda a, b: jnp.where(reached, a, b), new, before)  151 us
    psum x1, blocking collectives, on_device(): lax.psum((grad_weight, grad_bias, grad_dtb, grad_alog, grad_gain), ('dp',...  66 us
    psum x1, waiting for transfers between devices, on_device(): lax.psum((grad_weight, grad_bias, grad_dtb, grad_alog, grad_gain), ('dp',...  65.2 us
    dot_general x6, matrix products, scan_block(): output = jnp.einsum('hts,shp->thp', weights, values_x, precision=exact_mode)  46.7 us
    dot_general x8, matrix products, scan_block(): jnp.einsum('tn,hpn->thp', reads_c, carry_state, precision=exact_mode)  46.1 us
    dot_general x6, matrix products, scan_block(): jnp.einsum('shp,sn->hpn', leave_weight[:, :, None] * values_x, keys_b, pr...  37.8 us
    unnamed x97, local copies, waits for them, and re-layouts  28 us
  transfers between devices with their start and end apart: 5, of which 3 were waited for; matrix products, arithmetic and copies ran while one was open for 5% of the time, Pallas kernels for 0%

commit v1 on v0

--- a/solution.py
+++ b/solution.py
@@ -198,7 +198,9 @@
         ],
         axis=0,
     )
-    summed = lax.psum((grad_weight, grad_bias, grad_dtb, grad_alog, grad_gain), ("dp", "seq"))
+    summed = lax.psum(
+        lax.psum((grad_weight, grad_bias, grad_dtb, grad_alog, grad_gain), "seq"), "dp"
+    )
     scale = float(lax.axis_size("dp") * lax.axis_size("seq") * row_count) ** (-0.5)
     return (
         output,

time: 1140 us -> 1180 us (1.035)
  blocking collectives: 87.7 us -> 156 us
  waiting for transfers between devices: 489 us -> 463 us
    psum x1 -> x2, blocking collectives: 66 us -> 135 us  [the longest x1 121 us: on_device(): lax.psum((grad_weight, grad_bias, grad_dtb, grad_alog, grad_gain), 'seq')]
    psum x1 -> x2, waiting for transfers between devices: 65.2 us -> 38.9 us  [the longest x1 38.9 us: on_device(): lax.psum(lax.psum((grad_weight, grad_bias, grad_dtb, grad_alog, grad_gain...]
  transfers between devices with their start and end apart: 5 -> 6, of which waited for: 3 -> 3; matrix products, arithmetic and copies ran while one was open for 5% -> 5% of each run, Pallas kernels for 0% -> 0%
where the time goes in v1:
time: 1180 us
  waiting for transfers between devices  463 us (39%)
  other arithmetic  218 us (18%)
  blocking collectives  156 us (13%)
  matrix products  153 us (13%)
  local copies, waits for them, and re-layouts  151 us (13%)
  between operations  14.8 us (1%)
  loops' own time  12.2 us (1%)
    all_gather x2, waiting for transfers between devices, prefix(): everything = jax.tree.map(lambda part: lax.all_gather(part, axis), array)  424 us
    select_n x64, other arithmetic, step(): return jax.tree.map(lambda a, b: jnp.where(reached, a, b), new, before)  151 us
    psum x1, blocking collectives, on_device(): lax.psum((grad_weight, grad_bias, grad_dtb, grad_alog, grad_gain), 'seq')  121 us
    dot_general x6, matrix products, scan_block(): output = jnp.einsum('hts,shp->thp', weights, values_x, precision=exact_mode)  46.7 us
    dot_general x8, matrix products, scan_block(): jnp.einsum('tn,hpn->thp', reads_c, carry_state, precision=exact_mode)  46.1 us
    psum x1, waiting for transfers between devices, on_device(): lax.psum(lax.psum((grad_weight, grad_bias, grad_dtb, grad_alog, grad_gain...  38.9 us
    dot_general x6, matrix products, scan_block(): jnp.einsum('shp,sn->hpn', leave_weight[:, :, None] * values_x, keys_b, pr...  37.8 us
    unnamed x97, local copies, waits for them, and re-layouts  27.9 us
  transfers between devices with their start and end apart: 6, of which 3 were waited for; matrix products, arithmetic and copies ran while one was open for 5% of the time, Pallas kernels for 0%

profile of v1, /device:TPU:1, one launch (start us, length us, event | category | flops | bytes accessed | tf_op | source)
XLA Modules:
  0.0 1175.8 jit_solution(2728350878111553526)
XLA Ops:
  21.4 7.5 fusion.100
  36.5 69.3 %while.76 = (s32[]{:T(128)}, f32[80,64,128]{2,1,0:T(8,128)S(1)}, f32[2,64,80,64]{3,2,1,0:T(8,128)}, f32[2,80,64,128]{3,2,1,0:T(8,128)}, f32[2,80]{1,0:T(2,128)S(...) while((s32[]{:T(128)}, f32[80,64,128]{2,1,0:T(8,128)S(1)}, ...), condition=%wide.region_5.6_spmd.clone, body=%wide.region_2.5_spmd.clone.sunk | while | flops 1271495936 | bytes 43904780 | solution.py:109
  55.8 8.7 fusion.194
  90.4 8.7 fusion.194
  114.3 21.7 %all-gather.2 = f32[32,1,80]{2,1,0:T(1,128)S(1)} all-gather(f32[1,1,80]{2,1,0:T(1,128)S(1)} %multiply_bitcast_fusion), channel_id=1, replica_groups=mesh['dp'=4,'seq'=32] {'seq'}, dimensions={0}, use_global_device_ids=true | all-gather | bytes 10560 | tf_op jit(solution)/shard_map/all_gather | solution.py:23
  136.0 218.2 %all-gather.6.cloned.1.call-done = f32[2560,64,128]{2,1,0:T(8,128)} async-done(((f32[80,64,128]{2,1,0:T(8,128)}), f32[2560,64,128]{2,1,0:T(8,128)}) %all-gather.6.cloned.1.call-update) | async-done | bytes 83886096 | tf_op jit(solution)/shard_map/all_gather | solution.py:23
  354.3 77.1 %while.77 = (s32[]{:T(128)}, f32[80,64,128]{2,1,0:T(8,128)S(1)}, s32[]{:T(128)}, f32[32,80]{1,0:T(8,128)S(1)}, f32[32,80,64,128]{3,2,1,0:T(8,128)}, /*index=5*/s32[]{:T(128)}, s32[]{:T(128)}) while((s32[]{:T(128)}, f32[80,64,128]{2,1,0:T(8,128)S(1)}, s32[]{:T(128)}, f32[32,80]{1,0:T(8,128)S(1)}, f32[32,80,64,128]{3,2,1,0:T(8,128)}, ...), condition=%wide.region_8.9_spmd.clone, body=%wide.region_7.8_spmd.clone.sunk | while | flops 2621444 | bytes 7865393 | solution.py:36
  431.3 8.7 multiply_reduce_fusion.10
  452.7 8.1 copy.125
  460.8 6.5 copy.124
  484.9 205.6 %all-gather.8.cloned.1.call-done = f32[2560,64,128]{2,1,0:T(8,128)} async-done(((f32[80,64,128]{2,1,0:T(8,128)}), f32[2560,64,128]{2,1,0:T(8,128)}) %all-gather.8.cloned.1.call-update) | async-done | bytes 83886096 | tf_op jit(solution)/shard_map/all_gather | solution.py:23
  690.5 77.1 %while.78 = (s32[]{:T(128)}, f32[80,64,128]{2,1,0:T(8,128)S(1)}, s32[]{:T(128)}, f32[32,80]{1,0:T(8,128)S(1)}, f32[32,80,64,128]{3,2,1,0:T(8,128)}, /*index=5*/s32[]{:T(128)}, s32[]{:T(128)}, s32[]{:T(128)}, s32[]{:T(128)}) while((s32[]{:T(128)}, f32[80,64,128]{2,1,0:T(8,128)S(1)}, s32[]{:T(128)}, f32[32,80]{1,0:T(8,128)S(1)}, ...), condition=%wide.region_10.11_spmd.clone, body=%wide.region_9.10_spmd.clone.sunk | while | flops 2621448 | bytes 7865455 | solution.py:36
  772.6 176.2 %while.79 = (s32[]{:T(128)}, f32[80,64,128]{2,1,0:T(8,128)}, f32[80]{0:T(128)S(1)}, f32[2,64,80,64]{2,1,3,0:T(8,128)}, f32[2,64,128]{2,1,0:T(8,128)S(1)}, /*inde...) while((s32[]{:T(128)}, f32[80,64,128]{2,1,0:T(8,128)}, ...), condition=%wide.region_24.25_spmd.clone, body=%wide.region_11.24_spmd.clone.sunk | while | flops 3052656640 | bytes 114250048 | solution.py:109
  788.9 8.2 fusion.220
  797.3 9.1 multiply_reduce_fusion.17
  811.5 9.6 multiply_reduce_fusion.16
  836.9 6.5 fusion.219
  873.0 8.2 fusion.220
  881.4 9.1 multiply_reduce_fusion.17
  895.6 9.6 multiply_reduce_fusion.16
  960.4 7.3 fusion.110
  986.8 121.2 %all-reduce.15 = (f32[5376]{0:T(1024)S(1)}, f32[80]{0:T(128)S(1)}, f32[80]{0:T(128)S(1)}, f32[80]{0:T(128)S(1)}) all-reduce(f32[5376]{0:T(1024)S(1)} %get-tuple-element.978, f32[80]{0:T(128)S(1)} %get-tuple-element.981, f32[80]{0:T(128)S(1)} %negate_multiply_fusion, ...), channel_id=1, replica_groups=mesh['dp'=4,'seq'=32] {'seq'}, use_global_device_ids=true, to_apply=%region_32.33 | all-reduce | flops 5616 | bytes 44928 | tf_op jit(solution)/shard_map/psum | solution.py:202
  1108.0 13.4 %all-reduce.16 = (f32[5376]{0:T(1024)S(1)}, f32[80]{0:T(128)S(1)}, f32[80]{0:T(128)S(1)}, f32[80]{0:T(128)S(1)}) all-reduce(f32[5376]{0:T(1024)S(1)} %get-tuple-element.1064, f32[80]{0:T(128)S(1)} %get-tuple-element.1065, f32[80]{0:T(128)S(1)} %get-tuple-element.1066, ...), channel_id=1, replica_groups=mesh['dp'=4,'seq'=32] {'dp'}, use_global_device_ids=true, to_apply=%region_33.34 | all-reduce | flops 5616 | bytes 44928 | tf_op jit(solution)/shard_map/psum | solution.py:201
  1128.6 38.9 %all-reduce.22.cloned.1.call-done = f32[4,5376]{1,0:T(4,128)} async-done(((f32[4,5376]{1,0:T(4,128)}), f32[4,5376]{1,0:T(4,128)}) %all-reduce.22.cloned.1.call-update) | async-done | bytes 86032 | tf_op jit(solution)/shard_map/psum | solution.py:201
  (469 shorter events, 414.3 us)
Async XLA Ops:
  7.2 14.3 %copy-start.37 = (f32[5376]{0:T(1024)S(1)}, f32[5376]{0:T(1024)}, u32[]{:S(2)}) copy-start(f32[5376]{0:T(1024)} %param.20) | copy-start | bytes 64516
  7.2 347.1 %all-gather.6.cloned.1.call-start = ((), (), s32[]{:S(2)}) async-start(), calls=%async_computation.2 | async-start | bytes 86507520 | tf_op jit(solution)/shard_map/all_gather | solution.py:23
  9.4 12.0 %collective-permute-start = (bf16[3,5376]{1,0:T(4,128)(2,1)S(1)}, bf16[3,5376]{1,0:T(4,128)(2,1)S(1)}, u32[]{:S(2)}, u32[]{:S(2)}) collective-permute-start(bf16[3,5376]{1,0:T(4,128)(2,1)S(1)} %slice_multiply_fusion), channel_id=1, source_target_pairs={{0,1},{1,2},{2,3},{3,4},{4,5},{5,6},{6,7},{7,8},{8,9},{9,10},{10,1... | collective-permute-start | bytes 96776 | tf_op jit(solution)/shard_map/ppermute | solution.py:18
  14.9 14.0 %copy-start.26 = (f32[128,80]{1,0:T(8,128)}, f32[128,80]{1,0:T(8,128)S(1)}, u32[]{:S(2)}) copy-start(f32[128,80]{1,0:T(8,128)S(1)} %copy.111) | copy-start | bytes 122884
  16.1 12.8 %copy-start.39 = (f32[128]{0:T(128)}, f32[128]{0:T(128)S(1)}, u32[]{:S(2)}) copy-start(f32[128]{0:T(128)S(1)} %get-tuple-element.1107) | copy-start | bytes 1540
  16.1 12.8 %copy-start.41 = (f32[128]{0:T(128)}, f32[128]{0:T(128)S(1)}, u32[]{:S(2)}) copy-start(f32[128]{0:T(128)S(1)} %get-tuple-element.1108) | copy-start | bytes 1540
  16.1 12.9 %copy-start.43 = (f32[128]{0:T(128)}, f32[128]{0:T(128)S(1)}, u32[]{:S(2)}) copy-start(f32[128]{0:T(128)S(1)} %get-tuple-element.1109) | copy-start | bytes 1540
  16.1 97.4 %copy-start.45 = (f32[128]{0:T(128)}, f32[128]{0:T(128)S(1)}, u32[]{:S(2)}) copy-start(f32[128]{0:T(128)S(1)} %get-tuple-element.1106) | copy-start | bytes 1540
  18.1 10.8 copy-start.29
  18.1 10.8 copy-start.31
  18.2 10.8 copy-start.33
  18.2 10.8 copy-start.35
  21.4 7.6 copy-start.22
  107.3 583.2 %all-gather.8.cloned.1.call-start = ((), (), s32[]{:S(2)}) async-start(), calls=%async_computation.3 | async-start | bytes 86507520 | tf_op jit(solution)/shard_map/all_gather | solution.py:23
  112.9 241.4 %copy-start.24 = (f32[128,80]{1,0:T(8,128)}, f32[128,80]{1,0:T(8,128)S(1)}, u32[]{:S(2)}) copy-start(f32[128,80]{1,0:T(8,128)S(1)} %reduce_window_sum.84) | copy-start | bytes 122884
  431.3 8.7 copy-start.5
  446.6 679.1 %all-reduce.20.cloned.1.call-start = ((), (), s32[]{:S(2)}) async-start(), calls=%async_computation | async-start | bytes 172032 | tf_op jit(solution)/shard_map/psum | solution.py:202
  797.3 9.1 copy-start
  881.3 9.1 copy-start
  954.9 12.9 %copy-start.23 = (f32[3,5376]{1,0:T(4,128)S(1)}, f32[3,5376]{1,0:T(4,128)}, u32[]{:S(2)}) copy-start(f32[3,5376]{1,0:T(4,128)} %copy-done.22) | copy-start | bytes 193540
  981.1 144.7 %copy-start.13 = (f32[128,5376]{1,0:T(8,128)S(1)}, f32[128,5376]{1,0:T(8,128)}, u32[]{:S(2)}) copy-start(f32[128,5376]{1,0:T(8,128)} %copy-done.12) | copy-start | bytes 8257540
  981.1 144.7 %copy-start.51 = (f32[3]{0:T(128)S(1)}, f32[3]{0:T(128)}, u32[]{:S(2)}) copy-start(f32[3]{0:T(128)} %copy-done.50) | copy-start | bytes 40
  981.1 144.7 %collective-permute-start.1 = (f32[3,5376]{1,0:T(4,128)S(1)}, f32[3,5376]{1,0:T(4,128)S(1)}, u32[]{:S(2)}, u32[]{:S(2)}) collective-permute-start(f32[3,5376]{1,0:T(4,128)S(1)} %pad_add_fusion.1), channel_id=1, source_target_pairs={{1,0},{2,1},{3,2},{4,3},{5,4},{6,5},{7,6},{8,7},{9,8},{10,9},{11,1... | collective-permute-start | bytes 193544 | tf_op jit(solution)/shard_map/ppermute | solution.py:18
  984.4 183.0 %all-reduce.22.cloned.1.call-start = ((), (), s32[]{:S(2)}) async-start(), calls=%async_computation.1 | async-start | bytes 172032 | tf_op jit(solution)/shard_map/psum | solution.py:201
  (42 other events, 196.5 us)
Sparse Core Ops, SparseCore 0:
  107.4 246.8 all-gather.5
  446.8 243.7 all-gather.7
  984.5 96.2 all-reduce.19
  1125.9 41.4 all-reduce.21
